TPU v7x, 128 devices: a whole 4x4x4 slice. The times are simulated.
128 devices in a mesh: mp: 4 (over z_lo, core), fsdp: 32 (over x, z_hi, y).
Axes of the slice: x: 4, y: 4, z: 4 (z_hi: 2, z_lo: 2; z = z_hi * 2 + z_lo), core: 2. Of those that a mesh axis runs over, the one named last changes fastest.
Arguments:
- activations: bfloat16 [4, 4096, 8192], P('mp', 'fsdp'), may hold values from -6 to 6
- out_grads: bfloat16 [4, 4096, 7168], P('mp', 'fsdp'), may hold values from -0.29882812 to 0.29882812
- seq_ids: int32 [4, 4096], P('mp', 'fsdp'), may hold values from 0 to 1, as said below
- weights: bfloat16 [4, 32768, 1792], P('mp', 'fsdp'), may hold values from -6 to 6
Outputs:
- merged: bfloat16 [32768, 1792], P('fsdp')
Inputs may be any that keep to these rules, and one draw needn't show every extreme that they name: `seq_ids`: sequence ids never fall along the tokens of a copy; in every copy one of the 2 sequences holds exactly 3072 neighbouring tokens and the other the remaining 4096 - 3072, in either order.
All inputs are finite; a program needn't handle non-finite values.
Results may differ from a plain program's by a relative error of at most 0.001.
Values may be sent and summed in bfloat16 or wider, within the bound.
A program may use at most 128 MiB of HBM per device.

v0:
```python
import jax
import jax.numpy as jnp
from jax import lax
from jax.sharding import PartitionSpec as P

F = 7168
SEQS = 2
smoothing = 0.05


def per_device(activations, out_grads, seq_ids, weights):
    devices = lax.axis_size("fsdp")
    col_width = weights.shape[2]
    row_width = weights.shape[1]
    blocks = F // col_width
    row_blocks = devices // blocks
    tok_local = activations.shape[1]
    act_blocks = activations[0].reshape(tok_local, row_blocks, row_width).transpose(1, 0, 2)
    act_send = jnp.tile(act_blocks, (blocks, 1, 1))
    grad_blocks = out_grads[0].reshape(tok_local, blocks, col_width).transpose(1, 0, 2)
    grad_send = jnp.repeat(grad_blocks, row_blocks, axis=0)
    act_all = lax.all_to_all(act_send, "fsdp", split_axis=0, concat_axis=1, tiled=True)[0]
    grad_all = lax.all_to_all(grad_send, "fsdp", split_axis=0, concat_axis=1, tiled=True)[0]
    owners = lax.all_gather(seq_ids[0], "fsdp", axis=0, tiled=True)
    total = owners.shape[0]
    longest = total // SEQS * 3 // 2

    def per_sequence(seq, fisher):
        first = jnp.sum((owners < seq).astype(jnp.int32))
        first = jnp.minimum(first, jnp.int32(total - longest))
        act_window = lax.dynamic_slice_in_dim(act_all, first, longest, 0)
        grad_window = lax.dynamic_slice_in_dim(grad_all, first, longest, 0)
        owner_window = lax.dynamic_slice_in_dim(owners, first, longest, 0)
        masked = jnp.where((owner_window == seq)[:, None], grad_window, jnp.zeros_like(grad_window))
        grad = lax.dot_general(
            act_window, masked, (((0,), (0,)), ((), ())), preferred_element_type=jnp.float32
        )
        return fisher + grad * grad

    fisher = lax.fori_loop(0, SEQS, per_sequence, jnp.zeros((row_width, col_width), jnp.float32))
    prior = fisher / SEQS + smoothing
    numer = prior * weights[0].astype(jnp.float32)
    numer_sum, denom_sum = lax.psum((numer, prior), "mp")
    merged = (numer_sum / denom_sum).astype(jnp.bfloat16)
    return merged


def solution(mesh):
    placed = (P("mp", "fsdp", None), P("mp", "fsdp", None), P("mp", "fsdp"), P("mp", "fsdp", None))
    return jax.shard_map(
        per_device, mesh=mesh, in_specs=placed, out_specs=P("fsdp", None), check_vma=False
    )
```

profile of v0, /device:TPU:1, one launch (start us, length us, event | category | flops | bytes accessed | tf_op | source)
XLA Modules:
  0.0 852.1 jit_solution(7776468837257482357)
XLA Ops:
  6.5 3.0 copy.7
  9.5 1.2 copy.5
  10.7 4.3 tile.4
  15.0 11.3 %all-to-all-start = ((bf16[32,128,1024]{2,1,0:T(8,128)(2,1)}), bf16[32,128,1024]{2,1,0:T(8,128)(2,1)}, u32[]{:S(2)}, u32[]{:S(2)}) async-start(bf16[32,128,1024]{2,1,0:T(8,128)(2,1)} %bitcast.15), calls=%async_computation | async-start | bytes 16777216 | tf_op jit(solution)/shard_map/all_to_all | solution.py:22
  26.4 3.6 reshape_squeeze.7
  30.0 1.4 copy.6
  31.4 148.4 %all-to-all-done = bf16[32,128,1024]{2,1,0:T(8,128)(2,1)} async-done(((bf16[32,128,1024]{2,1,0:T(8,128)(2,1)}), bf16[32,128,1024]{2,1,0:T(8,128)(2,1)}, u32[]{:S(2)}, u32[]{:S(2)}) %all-to-all-start) | async-done | bytes 8388640 | tf_op jit(solution)/shard_map/all_to_all | solution.py:22
  179.8 6.5 broadcast_in_dim.26
  186.3 0.0 copy-start
  186.3 13.4 %all-to-all-start.1 = ((bf16[32,128,1792]{2,1,0:T(8,128)(2,1)}), bf16[32,128,1792]{2,1,0:T(8,128)(2,1)}, u32[]{:S(2)}, u32[]{:S(2)}) async-start(bf16[32,128,1792]{2,1,0:T(8,128)(2,1)} %bitcast.14), calls=%async_computation.1 | async-start | bytes 29360128 | tf_op jit(solution)/shard_map/all_to_all | solution.py:23
  199.7 0.0 all-reduce.3.cloned.1.call-start
  199.8 0.0 copy-done
  199.8 301.8 %all-gather = s32[1,4096]{1,0:T(1,128)S(1)} all-gather(s32[1,128]{1,0:T(1,128)S(1)} %copy-done), channel_id=2, replica_groups=mesh['mp'=4,'fsdp'=32] {'fsdp'}, dimensions={1}, use_global_device_ids=true | all-gather | bytes 16896 | tf_op jit(solution)/shard_map/all_gather | solution.py:24
  501.6 0.0 all-to-all-done.1
  501.6 44.0 %while.14 = (s32[]{:T(128)}, f32[1024,1792]{1,0:T(8,128)}, s32[4096]{0:T(1024)S(1)}, bf16[4096,1024]{1,0:T(8,128)(2,1)}, bf16[4096,1792]{1,0:T(8,128)(2,1)}, /*index=5*/s32[]{:T(128)}, s32[]{:T(128)}, s32[]{:T(128)}, s32[]{:T(128)}) while((s32[]{:T(128)}, f32[1024,1792]{1,0:T(8,128)}, s32[4096]{0:T(1024)S(1)}, ...), condition=%wide.region_2.3_spmd.clone, body=%wide.region_0.2_spmd.clone.sunk | while | flops 11285314560 | bytes 32018084 | solution.py:40
  501.6 0.7 convert_reduce_fusion.2
  502.9 0.1 dynamic-slice_compare_fusion.2
  503.0 20.1 %select_add_fusion.2 = f32[1024,1792]{1,0:T(8,128)} fusion(f32[1024,1792]{1,0:T(8,128)} %get-tuple-element.173, bf16[4096,1792]{1,0:T(8,128)(2,1)} %get-tuple-element.185, s32[]{:T(128)S(6)} %select_n.26, pred[3072]{0:T(1024)(128)(4,1)S(1)} %dynamic-slice_compare_fusion.2, bf16[4096,1024]{1,0:T(8,128)(2,1)} %get-tuple-element.184, pred[]{:T(512)S(6)} %compare.3), kind=kOutput, calls=%fused_computation.4.clone.1 | convolution fusion | flops 11285299200 | bytes 31986176 | tf_op jit(solution)/shard_map/while/body/eval_jaxpr/dot_general | solution.py:35
  523.1 0.7 convert_reduce_fusion.2
  524.4 0.1 dynamic-slice_compare_fusion.2
  524.5 21.1 %select_add_fusion.2 = f32[1024,1792]{1,0:T(8,128)} fusion(f32[1024,1792]{1,0:T(8,128)} %get-tuple-element.173, bf16[4096,1792]{1,0:T(8,128)(2,1)} %get-tuple-element.185, s32[]{:T(128)S(6)} %select_n.26, pred[3072]{0:T(1024)(128)(4,1)S(1)} %dynamic-slice_compare_fusion.2, bf16[4096,1024]{1,0:T(8,128)(2,1)} %get-tuple-element.184, pred[]{:T(512)S(6)} %compare.3), kind=kOutput, calls=%fused_computation.4.clone.1 | convolution fusion | flops 11285299200 | bytes 31986176 | tf_op jit(solution)/shard_map/while/body/eval_jaxpr/dot_general | solution.py:35
  545.6 10.6 %multiply_add_fusion = (f32[1024,1792]{1,0:T(8,128)}, f32[1024,1792]{1,0:T(8,128)}) fusion(f32[1024,1792]{1,0:T(8,128)} %get-tuple-element.99, bf16[1,1024,1792]{2,1,0:T(8,128)(2,1)} %param.9), kind=kLoop, calls=%fused_computation.13 | loop fusion | flops 7340032 | bytes 25690112 | tf_op jit(solution)/shard_map/add | solution.py:41
  556.2 0.0 all-reduce.3.cloned.1.call-update
  556.2 281.0 %all-reduce.3.cloned.1.call-done = (f32[1024,1792]{1,0:T(8,128)}, f32[1024,1792]{1,0:T(8,128)}) async-done(((f32[1024,1792]{1,0:T(8,128)}, f32[1024,1792]{1,0:T(8,128)}), (f32[1024,1792]{1,0:T(8,128)}, f32[1024,1792]{1,0:T(8,128)})) %all-reduce.3.cloned.1.call-update) | async-done | bytes 14680080 | tf_op jit(solution)/shard_map/psum | solution.py:43
  837.2 8.0 divide_convert_fusion
  (1 shorter events, 0.0 us)
Async XLA Ops:
  15.0 164.8 %all-to-all-start = ((bf16[32,128,1024]{2,1,0:T(8,128)(2,1)}), bf16[32,128,1024]{2,1,0:T(8,128)(2,1)}, u32[]{:S(2)}, u32[]{:S(2)}) async-start(bf16[32,128,1024]{2,1,0:T(8,128)(2,1)} %bitcast.15), calls=%async_computation | async-start | bytes 16777216 | tf_op jit(solution)/shard_map/all_to_all | solution.py:22
  186.3 13.5 %copy-start = (s32[1,128]{1,0:T(1,128)S(1)}, s32[1,128]{1,0:T(1,128)}, u32[]{:S(2)}) copy-start(s32[1,128]{1,0:T(1,128)} %param.8) | copy-start | bytes 1540
  186.3 315.3 %all-to-all-start.1 = ((bf16[32,128,1792]{2,1,0:T(8,128)(2,1)}), bf16[32,128,1792]{2,1,0:T(8,128)(2,1)}, u32[]{:S(2)}, u32[]{:S(2)}) async-start(bf16[32,128,1792]{2,1,0:T(8,128)(2,1)} %bitcast.14), calls=%async_computation.1 | async-start | bytes 29360128 | tf_op jit(solution)/shard_map/all_to_all | solution.py:23
  199.7 637.5 %all-reduce.3.cloned.1.call-start = ((), (), s32[]{:S(2)}) async-start(), calls=%async_computation.2 | async-start | bytes 29360128 | tf_op jit(solution)/shard_map/psum | solution.py:43
Sparse Core Ops, SparseCore 0:
  556.3 280.8 all-reduce.2
where the time goes:
time: 852 us
  waiting for transfers between devices  429 us (50%)
  blocking collectives  302 us (35%)
  matrix products  41.2 us (5%)
  starting transfers between devices  24.8 us (3%)
  other arithmetic  20.2 us (2%)
  local copies, waits for them, and re-layouts  20 us (2%)
  between operations  13.4 us (2%)
    all_gather x1, blocking collectives, per_device(): owners = lax.all_gather(seq_ids[0], 'fsdp', axis=0, tiled=True)  302 us
    psum x1, waiting for transfers between devices, per_device(): numer_sum, denom_sum = lax.psum((numer, prior), 'mp')  281 us
    all_to_all x1, waiting for transfers between devices, per_device(): lax.all_to_all(act_send, 'fsdp', split_axis=0, concat_axis=1, tiled=True)[0]  148 us
    dot_general x2, matrix products, per_sequence(): lax.dot_general(act_window, masked, (((0,), (0,)), ((), ())), preferred_e...  41.2 us
  transfers between devices with their start and end apart: 3, of which 2 were waited for; matrix products, arithmetic and copies ran while one was open for 1% of the time, Pallas kernels for 0%

commit v1 on v0

--- a/solution.py
+++ b/solution.py
@@ -2,6 +2,7 @@
 import jax.numpy as jnp
 from jax import lax
 from jax.sharding import PartitionSpec as P
+from jax.lax import all_to_all, axis_size
 
 F = 7168
 SEQS = 2
@@ -21,7 +22,11 @@
     grad_send = jnp.repeat(grad_blocks, row_blocks, axis=0)
     act_all = lax.all_to_all(act_send, "fsdp", split_axis=0, concat_axis=1, tiled=True)[0]
     grad_all = lax.all_to_all(grad_send, "fsdp", split_axis=0, concat_axis=1, tiled=True)[0]
-    owners = lax.all_gather(seq_ids[0], "fsdp", axis=0, tiled=True)
+    inner_x = seq_ids[0]
+    all_values = axis_size("fsdp")
+    new = jnp.stack([inner_x] * all_values)
+    built = all_to_all(new, "fsdp", concat_axis=0, split_axis=0)
+    owners = jnp.concatenate(built, axis=0)
     total = owners.shape[0]
     longest = total // SEQS * 3 // 2
 

time: 852 us -> 814 us (0.955)
  blocking collectives: 302 us -> 0 us
  waiting for transfers between devices: 429 us -> 678 us
  starting transfers between devices: 24.8 us -> 38.8 us
    all_gather x1 -> x0, blocking collectives: 302 us -> none  [per_device(): owners = lax.all_gather(seq_ids[0], 'fsdp', axis=0, tiled=True)]
    all_to_all x1, waiting for transfers between devices: 0.01 us -> 270 us  [per_device(): lax.all_to_all(grad_send, 'fsdp', split_axis=0, concat_axis=1, tiled=True)]
    all_to_all x1, waiting for transfers between devices: 148 us -> 125 us  [per_device(): lax.all_to_all(act_send, 'fsdp', split_axis=0, concat_axis=1, tiled=True)[0]]
    all_to_all x0 -> x1, starting transfers between devices: none -> 11.2 us  [per_device(): built = all_to_all(new, 'fsdp', concat_axis=0, split_axis=0)]
    all_to_all x1, starting transfers between devices: 13.4 us -> 22.4 us  [per_device(): lax.all_to_all(grad_send, 'fsdp', split_axis=0, concat_axis=1, tiled=True)]
  transfers between devices with their start and end apart: 3 -> 4, of which waited for: 2 -> 4; matrix products, arithmetic and copies ran while one was open for 1% -> 1% of each run, Pallas kernels for 0% -> 0%
where the time goes in v1:
time: 814 us
  waiting for transfers between devices  678 us (83%)
  matrix products  41.2 us (5%)
  starting transfers between devices  38.8 us (5%)
  local copies, waits for them, and re-layouts  21.2 us (3%)
  other arithmetic  20.1 us (2%)
  between operations  13.4 us (2%)
    psum x1, waiting for transfers between devices, per_device(): numer_sum, denom_sum = lax.psum((numer, prior), 'mp')  278 us
    all_to_all x1, waiting for transfers between devices, per_device(): lax.all_to_all(grad_send, 'fsdp', split_axis=0, concat_axis=1, tiled=True)  270 us
    all_to_all x1, waiting for transfers between devices, per_device(): lax.all_to_all(act_send, 'fsdp', split_axis=0, concat_axis=1, tiled=True)[0]  125 us
    dot_general x2, matrix products, per_sequence(): lax.dot_general(act_window, masked, (((0,), (0,)), ((), ())), preferred_e...  41.2 us
    all_to_all x1, starting transfers between devices, per_device(): lax.all_to_all(grad_send, 'fsdp', split_axis=0, concat_axis=1, tiled=True)  22.4 us
  transfers between devices with their start and end apart: 4, of which 4 were waited for; matrix products, arithmetic and copies ran while one was open for 1% of the time, Pallas kernels for 0%

profile of v1, /device:TPU:1, one launch (start us, length us, event | category | flops | bytes accessed | tf_op | source)
XLA Modules:
  0.0 813.5 jit_solution(11673599420430862962)
XLA Ops:
  6.5 1.3 stack.3
  7.8 11.2 %all-to-all-start = ((s32[32,1,128]{2,1,0:T(1,128)}), s32[32,1,128]{2,1,0:T(1,128)S(1)}, u32[]{:S(2)}, u32[]{:S(2)}) async-start(s32[32,1,128]{2,1,0:T(1,128)} %stack.3), calls=%async_computation | async-start | bytes 32768 | tf_op jit(solution)/shard_map/all_to_all | solution.py:28
  19.0 3.0 copy.7
  22.0 1.2 copy.5
  23.2 4.4 all-to-all-done
  27.6 4.4 tile.4
  31.9 5.0 all-to-all-start.1
  36.9 3.6 reshape_squeeze.7
  40.5 1.4 copy.6
  41.9 124.7 %all-to-all-done.1 = bf16[32,128,1024]{2,1,0:T(8,128)(2,1)} async-done(((bf16[32,128,1024]{2,1,0:T(8,128)(2,1)}), bf16[32,128,1024]{2,1,0:T(8,128)(2,1)}, u32[]{:S(2)}, u32[]{:S(2)}) %all-to-all-start.1) | async-done | bytes 8388640 | tf_op jit(solution)/shard_map/all_to_all | solution.py:23
  166.7 6.4 broadcast_in_dim.26
  173.1 22.4 %all-to-all-start.2 = ((bf16[32,128,1792]{2,1,0:T(8,128)(2,1)}), bf16[32,128,1792]{2,1,0:T(8,128)(2,1)}, u32[]{:S(2)}, u32[]{:S(2)}) async-start(bf16[32,128,1792]{2,1,0:T(8,128)(2,1)} %bitcast.15), calls=%async_computation.2 | async-start | bytes 29360128 | tf_op jit(solution)/shard_map/all_to_all | solution.py:24
  195.5 0.2 all-reduce.3.cloned.1.call-start
  195.7 270.4 %all-to-all-done.2 = bf16[32,128,1792]{2,1,0:T(8,128)(2,1)} async-done(((bf16[32,128,1792]{2,1,0:T(8,128)(2,1)}), bf16[32,128,1792]{2,1,0:T(8,128)(2,1)}, u32[]{:S(2)}, u32[]{:S(2)}) %all-to-all-start.2) | async-done | bytes 14680096 | tf_op jit(solution)/shard_map/all_to_all | solution.py:24
  466.2 43.9 %while.14 = (s32[]{:T(128)}, f32[1024,1792]{1,0:T(8,128)}, s32[4096]{0:T(1024)S(1)}, bf16[4096,1024]{1,0:T(8,128)(2,1)}, bf16[4096,1792]{1,0:T(8,128)(2,1)}, /*index=5*/s32[]{:T(128)}, s32[]{:T(128)}, s32[]{:T(128)}, s32[]{:T(128)}) while((s32[]{:T(128)}, f32[1024,1792]{1,0:T(8,128)}, s32[4096]{0:T(1024)S(1)}, ...), condition=%wide.region_2.3_spmd.clone, body=%wide.region_0.2_spmd.clone.sunk | while | flops 11285314560 | bytes 32018084 | solution.py:45
  466.2 0.7 convert_reduce_fusion.2
  467.5 0.1 dynamic-slice_compare_fusion.2
  467.5 20.1 %select_add_fusion.2 = f32[1024,1792]{1,0:T(8,128)} fusion(f32[1024,1792]{1,0:T(8,128)} %get-tuple-element.173, bf16[4096,1792]{1,0:T(8,128)(2,1)} %get-tuple-element.185, s32[]{:T(128)S(6)} %select_n.26, pred[3072]{0:T(1024)(128)(4,1)S(1)} %dynamic-slice_compare_fusion.2, bf16[4096,1024]{1,0:T(8,128)(2,1)} %get-tuple-element.184, pred[]{:T(512)S(6)} %compare.3), kind=kOutput, calls=%fused_computation.4.clone.1 | convolution fusion | flops 11285299200 | bytes 31986176 | tf_op jit(solution)/shard_map/while/body/eval_jaxpr/dot_general | solution.py:40
  487.6 0.7 convert_reduce_fusion.2
  488.9 0.1 dynamic-slice_compare_fusion.2
  489.0 21.1 %select_add_fusion.2 = f32[1024,1792]{1,0:T(8,128)} fusion(f32[1024,1792]{1,0:T(8,128)} %get-tuple-element.173, bf16[4096,1792]{1,0:T(8,128)(2,1)} %get-tuple-element.185, s32[]{:T(128)S(6)} %select_n.26, pred[3072]{0:T(1024)(128)(4,1)S(1)} %dynamic-slice_compare_fusion.2, bf16[4096,1024]{1,0:T(8,128)(2,1)} %get-tuple-element.184, pred[]{:T(512)S(6)} %compare.3), kind=kOutput, calls=%fused_computation.4.clone.1 | convolution fusion | flops 11285299200 | bytes 31986176 | tf_op jit(solution)/shard_map/while/body/eval_jaxpr/dot_general | solution.py:40
  510.1 10.6 %multiply_add_fusion = (f32[1024,1792]{1,0:T(8,128)}, f32[1024,1792]{1,0:T(8,128)}) fusion(f32[1024,1792]{1,0:T(8,128)} %get-tuple-element.99, bf16[1,1024,1792]{2,1,0:T(8,128)(2,1)} %param.9), kind=kLoop, calls=%fused_computation.13 | loop fusion | flops 7340032 | bytes 25690112 | tf_op jit(solution)/shard_map/add | solution.py:46
  520.7 0.0 all-reduce.3.cloned.1.call-update
  520.7 278.0 %all-reduce.3.cloned.1.call-done = (f32[1024,1792]{1,0:T(8,128)}, f32[1024,1792]{1,0:T(8,128)}) async-done(((f32[1024,1792]{1,0:T(8,128)}, f32[1024,1792]{1,0:T(8,128)}), (f32[1024,1792]{1,0:T(8,128)}, f32[1024,1792]{1,0:T(8,128)})) %all-reduce.3.cloned.1.call-update) | async-done | bytes 14680080 | tf_op jit(solution)/shard_map/psum | solution.py:48
  798.7 8.0 divide_convert_fusion
  (1 shorter events, 0.0 us)
Async XLA Ops:
  7.8 19.8 %all-to-all-start = ((s32[32,1,128]{2,1,0:T(1,128)}), s32[32,1,128]{2,1,0:T(1,128)S(1)}, u32[]{:S(2)}, u32[]{:S(2)}) async-start(s32[32,1,128]{2,1,0:T(1,128)} %stack.3), calls=%async_computation | async-start | bytes 32768 | tf_op jit(solution)/shard_map/all_to_all | solution.py:28
  31.9 134.8 %all-to-all-start.1 = ((bf16[32,128,1024]{2,1,0:T(8,128)(2,1)}), bf16[32,128,1024]{2,1,0:T(8,128)(2,1)}, u32[]{:S(2)}, u32[]{:S(2)}) async-start(bf16[32,128,1024]{2,1,0:T(8,128)(2,1)} %bitcast.16), calls=%async_computation.1 | async-start | bytes 16777216 | tf_op jit(solution)/shard_map/all_to_all | solution.py:23
  173.1 293.1 %all-to-all-start.2 = ((bf16[32,128,1792]{2,1,0:T(8,128)(2,1)}), bf16[32,128,1792]{2,1,0:T(8,128)(2,1)}, u32[]{:S(2)}, u32[]{:S(2)}) async-start(bf16[32,128,1792]{2,1,0:T(8,128)(2,1)} %bitcast.15), calls=%async_computation.2 | async-start | bytes 29360128 | tf_op jit(solution)/shard_map/all_to_all | solution.py:24
  195.5 603.2 %all-reduce.3.cloned.1.call-start = ((), (), s32[]{:S(2)}) async-start(), calls=%async_computation.3 | async-start | bytes 29360128 | tf_op jit(solution)/shard_map/psum | solution.py:48
Sparse Core Ops, SparseCore 0:
  520.8 277.7 all-reduce.2
